TPU v7x, 32 devices: a whole 2x2x4 slice. The times are simulated.
32 devices in a mesh: gx: 16 (over z, y, x), gy: 2 (over core).
Axes of the slice: x: 2, y: 2, z: 4, core: 2. Of those that a mesh axis runs over, the one named last changes fastest.
Arguments:
- density: float32 [128, 32, 64], P('gx', None, 'gy'), may hold values from 0.5 to 1.5
- momentum: float32 [3, 128, 32, 64], P(None, 'gx', None, 'gy'), may hold values from -3 to 3
- energy: float32 [128, 32, 64], P('gx', None, 'gy'), may hold values from 2.5 to 4
- eddy_normal_cell: int32 [1024], P('gx'), may hold values from 0 to 63
- eddy_spanwise_cell: int32 [1024], P('gx'), may hold values from 0 to 31
- eddy_signs: int32 [1024, 3], P('gx'), may hold values from 0 to 1
- eddy_strengths: float32 [1024], P('gx'), may hold values from 0.3 to 3
- filter_matrices: float32 [1, 128, 128], replicated, may hold values from -1.25 to 1.25
- shock_switch: int32 [1, 64], P(None, 'gy'), may hold values 0 or 1
- dilatation_bin: int32 [128, 32, 64], P('gx', None, 'gy'), may hold values from 0 to 63
- vorticity_bin: int32 [128, 32, 64], P('gx', None, 'gy'), may hold values from 0 to 63, as said below
Outputs:
- conserved_next: float32 [5, 128, 32, 64], P(None, 'gx', None, 'gy')
- histogram: float32 [64, 64], replicated
Inputs may be any that keep to these rules, and one draw needn't show every extreme that they name: vorticity_bin at streamwise cell x is x * 64 // 128 or one more, modulo 64.
All inputs are finite; a program needn't handle non-finite values. No bound on the sum of `shock_switch` on one device may be relied on, other than what follows from the above.
Results may differ from a plain program's by a relative error of at most 0.0003.
Values sent between devices are 32-bit elements; how exact they have to be, the bound alone decides.
No kernel may reach another device: no remote copies, remote signals or barrier semaphores. Data moves between devices by JAX's collectives and lax.ppermute only.
A program may use at most 64 MiB of HBM per device.

v0:
```python
import math
import jax
import jax.numpy as jnp
from jax import lax
from jax.sharding import PartitionSpec as P

HISTOGRAM_BINS = 64
SIGMA_Y = 32
SIGMA_Z = 8
TIME_STEP = 0.1
GAMMA_GAS = 1.4
SENSOR_EPS = 0.1
HAT_PEAK = math.sqrt(1.5)


def extended(x, sides, width):
    for axis, dim in sides:
        size, length = (lax.axis_size(axis), x.shape[dim])
        up = [(i, (i + 1) % size) for i in range(size - 1)]
        down = [(j, i) for i, j in up]
        last = lax.slice_in_dim(x, length - width, length, axis=dim)
        first = lax.slice_in_dim(x, 0, width, axis=dim)
        before = lax.ppermute(last, axis, up)
        after = lax.ppermute(first, axis, down)
        x = jnp.concatenate([before, x, after], axis=dim)
    return x


def hat_shape(centres, coords, spread, period):
    offset = coords[None, :] - centres[:, None]
    if period > 0:
        offset = jnp.mod(offset + period / 2, period) - period / 2
    return HAT_PEAK * jnp.maximum(0.0, 1.0 - jnp.abs(offset) / spread)


def inflow_from(centre_y, centre_z, eddy_weight, coords_y, coords_z, span):
    shape_y = hat_shape(centre_y, coords_y, float(SIGMA_Y), 0)
    shape_z = hat_shape(centre_z, coords_z, float(SIGMA_Z), span)
    weighted = (eddy_weight[:, :, None] * shape_z[:, None, :]).reshape(eddy_weight.shape[0], -1)
    inflow = jnp.dot(weighted.T, shape_y, precision=lax.Precision.HIGHEST)
    return inflow.reshape(3, coords_z.shape[0], coords_y.shape[0])


def ghost_state(inflow):
    mom_x = 1.0 + inflow[0]
    kinetic = mom_x * mom_x + inflow[1] * inflow[1] + inflow[2] * inflow[2]
    return jnp.stack([jnp.ones_like(mom_x), mom_x, inflow[1], inflow[2], 3.0 + 0.5 * kinetic])


def flux_of(fields, velocity, pressure, direction):
    result = fields * velocity[direction][None]
    result = result.at[1 + direction].add(pressure)
    return result.at[4].add(pressure * velocity[direction])


def central_x(values):
    return (values[..., 2:, :, 1:-1] - values[..., :-2, :, 1:-1]) * 0.5


def central_y(values):
    return (values[..., 1:-1, :, 2:] - values[..., 1:-1, :, :-2]) * 0.5


def central_z(values):
    centre = values[..., 1:-1, :, 1:-1]
    return (jnp.roll(centre, -1, axis=-2) - jnp.roll(centre, 1, axis=-2)) * 0.5


def section_rhs(padded):
    velocity = padded[1:4] / padded[0][None]
    pressure = (GAMMA_GAS - 1.0) * (padded[4] - 0.5 * jnp.sum(padded[1:4] * velocity, axis=0))
    change = central_x(flux_of(padded, velocity, pressure, 0))
    change = change + central_y(flux_of(padded, velocity, pressure, 1))
    change = change + central_z(flux_of(padded, velocity, pressure, 2))
    updated = padded[:, 1:-1, :, 1:-1] - TIME_STEP * change
    dilatation = central_x(velocity[0]) + central_y(velocity[1]) + central_z(velocity[2])
    vort_x = central_y(velocity[2]) - central_z(velocity[1])
    vort_y = central_z(velocity[0]) - central_x(velocity[2])
    vort_z = central_x(velocity[1]) - central_y(velocity[0])
    squared = dilatation * dilatation
    shock_sensor = squared / (
        squared + vort_x * vort_x + vort_y * vort_y + vort_z * vort_z + SENSOR_EPS
    )
    return (updated, shock_sensor)


def filter_lines(pencil, filter_matrices):
    block_count, block_len = (filter_matrices.shape[0], filter_matrices.shape[1])
    lanes = pencil.shape[2]
    blocks = pencil.reshape(5, block_count, block_len, lanes)
    smooth = jnp.einsum("bij,fbjp->fbip", filter_matrices, blocks, precision=lax.Precision.HIGHEST)
    return smooth.reshape(5, block_count * block_len, lanes)


def plane_histogram(shock_sensor, dilatation_bin, vorticity_bin):
    bin_levels = jnp.arange(HISTOGRAM_BINS, dtype=jnp.int32)

    def accumulate_plane(histogram_totals, histogram_parts):
        sensor_plane, plane_dilatation, plane_vorticity = histogram_parts
        flat_sensor = sensor_plane.reshape(-1)
        dilatation_table = (plane_dilatation.reshape(-1)[None, :] == bin_levels[:, None]).astype(
            jnp.float32
        )
        vorticity_table = jnp.where(
            plane_vorticity.reshape(-1)[:, None] == bin_levels[None, :], flat_sensor[:, None], 0.0
        )
        return (
            histogram_totals
            + jnp.dot(dilatation_table, vorticity_table, precision=lax.Precision.HIGHEST),
            None,
        )

    histogram_totals, _ = lax.scan(
        accumulate_plane,
        jnp.zeros((HISTOGRAM_BINS, HISTOGRAM_BINS), jnp.float32),
        (shock_sensor, dilatation_bin, vorticity_bin),
    )
    return histogram_totals


def shards(
    density,
    momentum,
    energy,
    eddy_normal_cell,
    eddy_spanwise_cell,
    eddy_signs,
    eddy_strengths,
    filter_matrices,
    shock_switch,
    dilatation_bin,
    vorticity_bin,
):
    cells_x, span, cells_y = density.shape
    slab_index = lax.axis_index("gx")
    block_index = lax.axis_index("gy")
    slab_count = lax.axis_size("gx")
    fields = jnp.concatenate([density[None], momentum, energy[None]], axis=0)
    total_y = cells_y * lax.axis_size("gy")
    total_eddies = eddy_normal_cell.shape[0] * slab_count
    amplitude = math.sqrt(total_y * span / (total_eddies * SIGMA_Y * SIGMA_Z))
    eddy_weight = (2 * eddy_signs - 1).astype(jnp.float32) * eddy_strengths[:, None] * amplitude
    coords_y = (block_index * cells_y + jnp.arange(cells_y, dtype=jnp.int32)).astype(jnp.float32)
    coords_z = jnp.arange(span, dtype=jnp.int32).astype(jnp.float32)
    partial_sum = inflow_from(
        eddy_normal_cell.astype(jnp.float32),
        eddy_spanwise_cell.astype(jnp.float32),
        eddy_weight,
        coords_y,
        coords_z,
        span,
    )
    inflow = lax.psum(partial_sum, "gx")
    ghost_cells = ghost_state(inflow)
    padded = extended(fields, (("gx", 1), ("gy", 3)), 1)
    padded = padded.at[:, 0, :, 1:-1].set(
        jnp.where(slab_index == 0, ghost_cells, padded[:, 0, :, 1:-1])
    )
    padded = padded.at[:, -1, :, 1:-1].set(
        jnp.where(slab_index == slab_count - 1, fields[:, -1], padded[:, -1, :, 1:-1])
    )
    padded = padded.at[:, 1:-1, :, 0].set(
        jnp.where(block_index == 0, fields[:, :, :, 0], padded[:, 1:-1, :, 0])
    )
    padded = padded.at[:, 1:-1, :, -1].set(
        jnp.where(
            block_index == lax.axis_size("gy") - 1, fields[:, :, :, -1], padded[:, 1:-1, :, -1]
        )
    )
    updated, shock_sensor = section_rhs(padded)
    block_len = filter_matrices.shape[1]
    filter_row = slab_index * cells_x // block_len
    mask_row = lax.dynamic_slice_in_dim(shock_switch, filter_row, 1, 0).astype(jnp.float32)
    weight = mask_row[None] * shock_sensor
    columns = span * cells_y
    stacked = updated.reshape(5, cells_x, columns)
    weight_flat = weight.reshape(1, cells_x, columns)
    pencil, pencil_weight = (
        lax.all_to_all(stacked, "gx", split_axis=2, concat_axis=1, tiled=True),
        lax.all_to_all(weight_flat, "gx", split_axis=2, concat_axis=1, tiled=True),
    )
    smooth = filter_lines(pencil, filter_matrices)
    returned = pencil + pencil_weight * (smooth - pencil)
    back_lines = lax.all_to_all(returned, "gx", split_axis=1, concat_axis=2, tiled=True)
    conserved_next = back_lines.reshape(5, cells_x, span, cells_y)
    partial_histogram = plane_histogram(shock_sensor, dilatation_bin, vorticity_bin)
    summed = lax.psum(partial_histogram, ("gx", "gy"))
    all_cells = cells_x * slab_count * span * total_y
    histogram = summed * (HISTOGRAM_BINS * HISTOGRAM_BINS / all_cells)
    return (conserved_next, histogram)


def solution(mesh):
    in_specs = (
        P("gx", None, "gy"),
        P(None, "gx", None, "gy"),
        P("gx", None, "gy"),
        P("gx"),
        P("gx"),
        P("gx", None),
        P("gx"),
        P(),
        P(None, "gy"),
        P("gx", None, "gy"),
        P("gx", None, "gy"),
    )
    out_specs = (P(None, "gx", None, "gy"), P())
    return jax.shard_map(shards, mesh=mesh, in_specs=in_specs, out_specs=out_specs, check_vma=False)
```

profile of v0, /device:TPU:0, one launch (start us, length us, event | category | flops | bytes accessed | tf_op | source)
XLA Modules:
  0.0 215.9 jit_solution(9551707045615207745)
XLA Ops:
  0.6 0.9 pad_maximum_fusion.4
  1.6 1.3 collective-permute-start.1
  2.9 5.5 %collective-permute-start = (f32[5,1,32,32]{3,2,0,1:T(8,128)S(1)}, f32[5,1,32,32]{3,2,0,1:T(8,128)S(1)}, u32[]{:S(2)}, u32[]{:S(2)}) collective-permute-start(f32[5,1,32,32]{3,2,0,1:T(8,128)S(1)} %get-tuple-element.222), channel_id=1, source_target_pairs={{0,2},{2,4},{4,6},{6,8},{8,10},{10,12},{12,14},{14,16},{16,18},{18... | collective-permute-start | bytes 61448 | tf_op jit(solution)/shard_map/ppermute | solution.py:23
  8.4 0.7 convert_element_type.33
  9.1 0.7 convert_element_type.31
  9.7 0.7 multiply_multiply_fusion
  10.8 75.6 %psum.14 = f32[3,32,32]{2,1,0:T(8,128)S(1)} all-reduce(f32[3,32,32]{2,1,0:T(8,128)S(1)} %fusion.50), channel_id=1, replica_groups=mesh['gx'=16,'gy'=2] {'gx'}, use_global_device_ids=true, to_apply=%region_1.2 | all-reduce | flops 3072 | bytes 24576 | tf_op jit(solution)/shard_map/psum | solution.py:153
  86.4 1.2 pad_maximum_fusion.2
  87.6 0.7 convert_bitcast_fusion
  88.4 0.6 slice.495
  88.9 1.2 pad_maximum_fusion
  91.2 1.3 collective-permute-start.3
  92.5 3.0 %collective-permute-start.2 = (f32[5,10,32,1]{2,3,1,0:T(1,128)S(1)}, f32[5,10,32,1]{2,3,1,0:T(1,128)S(1)}, u32[]{:S(2)}, u32[]{:S(2)}) collective-permute-start(f32[5,10,32,1]{2,3,1,0:T(1,128)S(1)} %copy.81), channel_id=1, source_target_pairs={{0,1},{2,3},{4,5},{6,7},{8,9},{10,11},{12,13},{14,15},{16,17},{18,... | collective-permute-start | bytes 19208 | tf_op jit(solution)/shard_map/ppermute | solution.py:23
  95.5 1.4 and_reduce_fusion
  96.9 0.4 copy.83
  97.3 1.3 copy.84
  98.6 1.6 pad_maximum_fusion.1
  100.2 1.4 fusion.48
  101.6 1.7 scatter.14
  103.4 1.0 scatter.15
  104.5 0.9 scatter.16
  105.4 0.4 slice_select_fusion
  105.9 3.7 %scatter.19 = f32[5,10,32,34]{3,2,0,1:T(8,128)S(1)} dynamic-update-slice(f32[5,10,32,34]{3,2,0,1:T(8,128)S(1)} %scatter.16, f32[5,8,32,1]{3,2,0,1:T(8,128)S(1)} %slice_select_fusion, s32[]{:T(128)} %constant.328.clone.1, s32[]{:T(128)} %constant.350.clone.1, s32[]{:T(128)} %constant.328.clone.1, s32[]{:T(128)} %constant.351.clone.1) | dynamic-update-slice | bytes 10244 | tf_op jit(solution)/shard_map/scatter | solution.py:165
  111.2 1.2 fusion.91
  112.4 0.4 broadcast_multiply_fusion.3
  112.8 1.0 copy.119
  113.9 0.5 broadcast.273
  114.4 3.7 %reduce.27 = f32[1024,8]{1,0:T(8,128)} reduce(f32[1024,1,8]{2,1,0:T(1,128)} %bitcast.128, f32[]{:T(128)} %broadcast.273), dimensions={1}, to_apply=%bitcast.110.reduce_sub_computation | reduce | bytes 65540
  118.1 1.9 reshape.467
  120.0 3.5 %all-to-all-start.1 = ((f32[16,1,512]{2,1,0:T(1,128)}), f32[16,1,512]{2,1,0:T(1,128)S(1)}, u32[]{:S(2)}, u32[]{:S(2)}) async-start(f32[16,1,512]{2,1,0:T(1,128)} %reshape.467), calls=%async_computation.1 | async-start | bytes 65536 | tf_op jit(solution)/shard_map/all_to_all | solution.py:180
  123.5 2.7 %fusion.14 = f32[5,8,32,32]{3,2,0,1:T(8,128)} fusion(f32[5,10,32,34]{3,2,0,1:T(8,128)S(1)} %get-tuple-element.221, f32[5,10,32,34]{3,2,0,1:T(8,128)S(1)} %scatter.19, f32[5,8,1,32]{3,2,0,1:T(1,128)S(1)} %get-tuple-element.213, f32[5,8,31,32]{3,2,0,1:T(8,128)} %get-tuple-element.215, f32[5,8,31,32]{3,2,0,1:T(8,128)S(1)} %get-tuple-element.214, ...), kind=kLoop, calls=%fused_computation.23 | loop fusion | flops 368640 | bytes 4295680 | tf_op jit(solution)/shard_map/sub | solution.py:75
  126.2 3.6 %copy.122 = f32[5,8,32,32]{1,0,3,2:T(8,128)} copy(f32[5,8,32,32]{3,2,0,1:T(8,128)} %fusion.14) | data formatting | bytes 327680 | tf_op jit(solution)/shard_map/reshape | solution.py:176
  129.8 3.4 %reshape.465 = f32[16,1,2560]{2,1,0:T(1,128)} reshape(f32[1024,5,8]{2,1,0:T(8,128)} %bitcast.117) | data formatting | bytes 327680
  133.1 6.9 %all-to-all-start = ((f32[16,1,2560]{2,1,0:T(1,128)}), f32[16,1,2560]{2,1,0:T(1,128)S(1)}, u32[]{:S(2)}, u32[]{:S(2)}) async-start(f32[16,1,2560]{2,1,0:T(1,128)} %reshape.465), calls=%async_computation | async-start | bytes 327680 | tf_op jit(solution)/shard_map/all_to_all | solution.py:179
  140.0 0.6 reduce.28
  140.7 0.9 reshape.468
  141.8 6.1 %all-to-all-done = f32[16,1,2560]{2,1,0:T(1,128)S(1)} async-done(((f32[16,1,2560]{2,1,0:T(1,128)}), f32[16,1,2560]{2,1,0:T(1,128)S(1)}, u32[]{:S(2)}, u32[]{:S(2)}) %all-to-all-start) | async-done | bytes 163872 | tf_op jit(solution)/shard_map/all_to_all | solution.py:179
  147.9 0.9 reduce.26
  148.9 2.6 %reshape.466 = f32[1024,5,8]{2,1,0:T(8,128)} reshape(f32[16,2560]{1,0:T(8,128)S(1)} %reduce.26) | data formatting | bytes 327680
  151.5 2.6 %copy.103 = f32[5,16,8,64]{3,2,1,0:T(8,128)S(1)} copy(f32[5,16,8,64]{2,0,3,1:T(8,128)} %bitcast.118) | data formatting | bytes 327680 | tf_op jit(solution)/shard_map/all_to_all | solution.py:179
  154.2 0.7 fusion.10
  155.2 0.9 reshape.469
  156.1 3.5 %all-to-all-start.2 = ((f32[16,1,2560]{2,1,0:T(1,128)}), f32[16,1,2560]{2,1,0:T(1,128)S(1)}, u32[]{:S(2)}, u32[]{:S(2)}) async-start(f32[16,1,2560]{2,1,0:T(1,128)} %reshape.469), calls=%async_computation.2 | async-start | bytes 327680 | tf_op jit(solution)/shard_map/all_to_all | solution.py:184
  159.6 12.6 %while.22 = (s32[]{:T(128)}, f32[64,64]{1,0:T(8,128)S(1)}, s32[8,32,32]{2,1,0:T(8,128)}, s32[8,32,32]{2,1,0:T(8,128)}, f32[8,32,32]{2,1,0:T(8,128)S(1)}, /*index=5*/s32[]{:T(128)}, s32[]{:T(128)}) while((s32[]{:T(128)}, f32[64,64]{1,0:T(8,128)S(1)}, s32[8,32,32]{2,1,0:T(8,128)}, s32[8,32,32]{2,1,0:T(8,128)}, ...), condition=%wide.region_4.5_spmd.clone.clone, body=%wide.region_3.4_spmd.clone.clone.sunk | while | flops 50536448 | bytes 94311 | solution.py:113
  159.7 0.7 constant_dynamic-slice_fusion.6
  160.6 0.6 convolution_add_fusion.2
  161.3 0.7 constant_dynamic-slice_fusion.6
  162.2 0.6 convolution_add_fusion.2
  162.8 0.7 constant_dynamic-slice_fusion.6
  163.7 0.6 convolution_add_fusion.2
  164.4 0.7 constant_dynamic-slice_fusion.6
  165.3 0.6 convolution_add_fusion.2
  166.0 0.7 constant_dynamic-slice_fusion.6
  166.9 0.6 convolution_add_fusion.2
  167.6 0.7 constant_dynamic-slice_fusion.6
  168.5 0.6 convolution_add_fusion.2
  169.1 0.7 constant_dynamic-slice_fusion.6
  170.0 0.6 convolution_add_fusion.2
  170.7 0.7 constant_dynamic-slice_fusion.6
  171.6 0.6 convolution_add_fusion.2
  172.2 40.8 %psum.15 = f32[64,64]{1,0:T(8,128)S(1)} all-reduce(f32[64,64]{1,0:T(8,128)S(1)} %get-tuple-element.157), channel_id=1, replica_groups=mesh['gx'=16,'gy'=2] {'gx','gy'}, use_global_device_ids=true, to_apply=%region_5.6 | all-reduce | flops 4096 | bytes 32768 | tf_op jit(solution)/shard_map/psum | solution.py:187
  213.0 0.6 broadcast_multiply_fusion.4
  213.6 0.9 reduce.29
  214.9 1.0 reshape.460
  (85 shorter events, 6.0 us)
Async XLA Ops:
  0.6 153.6 %copy-start = (f32[1,128,128]{2,1,0:T(8,128)S(1)}, f32[1,128,128]{2,1,0:T(8,128)}, u32[]{:S(2)}) copy-start(f32[1,128,128]{2,1,0:T(8,128)} %param.40) | copy-start | bytes 196612
  1.6 93.9 %copy-start.4 = (s32[4]{0:T(128)S(1)}, s32[4]{0:T(128)}, u32[]{:S(2)}) copy-start(s32[4]{0:T(128)} %constant.330.clone.1) | copy-start | bytes 52
  1.6 87.3 %collective-permute-start.1 = (f32[5,1,32,32]{3,2,0,1:T(8,128)S(1)}, f32[5,1,32,32]{3,2,0,1:T(8,128)S(1)}, u32[]{:S(2)}, u32[]{:S(2)}) collective-permute-start(f32[5,1,32,32]{3,2,0,1:T(8,128)S(1)} %get-tuple-element.223), channel_id=1, source_target_pairs={{2,0},{4,2},{6,4},{8,6},{10,8},{12,10},{14,12},{16,14},{18,16},{20... | collective-permute-start | bytes 61448 | tf_op jit(solution)/shard_map/ppermute | solution.py:24
  2.9 86.0 %collective-permute-start = (f32[5,1,32,32]{3,2,0,1:T(8,128)S(1)}, f32[5,1,32,32]{3,2,0,1:T(8,128)S(1)}, u32[]{:S(2)}, u32[]{:S(2)}) collective-permute-start(f32[5,1,32,32]{3,2,0,1:T(8,128)S(1)} %get-tuple-element.222), channel_id=1, source_target_pairs={{0,2},{2,4},{4,6},{6,8},{8,10},{10,12},{12,14},{14,16},{16,18},{18... | collective-permute-start | bytes 61448 | tf_op jit(solution)/shard_map/ppermute | solution.py:23
  87.6 11.0 %copy-start.1 = (f32[3,8,32,32]{3,2,1,0:T(8,128)S(1)}, f32[3,8,32,32]{3,2,1,0:T(8,128)}, u32[]{:S(2)}) copy-start(f32[3,8,32,32]{3,2,1,0:T(8,128)} %param.34) | copy-start | bytes 294916
  87.6 11.0 %copy-start.2 = (f32[8,32,32]{2,1,0:T(8,128)S(1)}, f32[8,32,32]{2,1,0:T(8,128)}, u32[]{:S(2)}) copy-start(f32[8,32,32]{2,1,0:T(8,128)} %param.35) | copy-start | bytes 98308
  87.6 11.0 %copy-start.3 = (f32[8,32,32]{2,1,0:T(8,128)S(1)}, f32[8,32,32]{2,1,0:T(8,128)}, u32[]{:S(2)}) copy-start(f32[8,32,32]{2,1,0:T(8,128)} %param.33) | copy-start | bytes 98308
  91.2 6.1 %collective-permute-start.3 = (f32[5,10,32,1]{2,3,1,0:T(1,128)S(1)}, f32[5,10,32,1]{2,3,1,0:T(1,128)S(1)}, u32[]{:S(2)}, u32[]{:S(2)}) collective-permute-start(f32[5,10,32,1]{2,3,1,0:T(1,128)S(1)} %copy.82), channel_id=1, source_target_pairs={{1,0},{3,2},{5,4},{7,6},{9,8},{11,10},{13,12},{15,14},{17,16},{19,... | collective-permute-start | bytes 19208 | tf_op jit(solution)/shard_map/ppermute | solution.py:24
  92.5 4.4 %collective-permute-start.2 = (f32[5,10,32,1]{2,3,1,0:T(1,128)S(1)}, f32[5,10,32,1]{2,3,1,0:T(1,128)S(1)}, u32[]{:S(2)}, u32[]{:S(2)}) collective-permute-start(f32[5,10,32,1]{2,3,1,0:T(1,128)S(1)} %copy.81), channel_id=1, source_target_pairs={{0,1},{2,3},{4,5},{6,7},{8,9},{10,11},{12,13},{14,15},{16,17},{18,... | collective-permute-start | bytes 19208 | tf_op jit(solution)/shard_map/ppermute | solution.py:23
  120.0 13.2 %all-to-all-start.1 = ((f32[16,1,512]{2,1,0:T(1,128)}), f32[16,1,512]{2,1,0:T(1,128)S(1)}, u32[]{:S(2)}, u32[]{:S(2)}) async-start(f32[16,1,512]{2,1,0:T(1,128)} %reshape.467), calls=%async_computation.1 | async-start | bytes 65536 | tf_op jit(solution)/shard_map/all_to_all | solution.py:180
  133.1 14.8 %all-to-all-start = ((f32[16,1,2560]{2,1,0:T(1,128)}), f32[16,1,2560]{2,1,0:T(1,128)S(1)}, u32[]{:S(2)}, u32[]{:S(2)}) async-start(f32[16,1,2560]{2,1,0:T(1,128)} %reshape.465), calls=%async_computation | async-start | bytes 327680 | tf_op jit(solution)/shard_map/all_to_all | solution.py:179
  156.1 57.5 %all-to-all-start.2 = ((f32[16,1,2560]{2,1,0:T(1,128)}), f32[16,1,2560]{2,1,0:T(1,128)S(1)}, u32[]{:S(2)}, u32[]{:S(2)}) async-start(f32[16,1,2560]{2,1,0:T(1,128)} %reshape.469), calls=%async_computation.2 | async-start | bytes 327680 | tf_op jit(solution)/shard_map/all_to_all | solution.py:184
where the time goes:
time: 218 us; the launch traced here: 216 us
  blocking collectives  116 us (53%)
  local copies, waits for them, and re-layouts  39.7 us (18%)
  starting transfers between devices  25 us (11%)
  other arithmetic  21.8 us (10%)
  waiting for transfers between devices  6.13 us (3%)
  matrix products  5.55 us (3%)
    psum x1, blocking collectives, shards(): inflow = lax.psum(partial_sum, 'gx')  75.6 us
    psum x1, blocking collectives, shards(): summed = lax.psum(partial_histogram, ('gx', 'gy'))  40.8 us
    unnamed x16, local copies, waits for them, and re-layouts  9.82 us
    ppermute x2, starting transfers between devices, extended(): before = lax.ppermute(last, axis, up)  8.5 us
    all_to_all x1, starting transfers between devices, shards(): lax.all_to_all(stacked, 'gx', split_axis=2, concat_axis=1, tiled=True)  6.88 us
    all_to_all x1, waiting for transfers between devices, shards(): lax.all_to_all(stacked, 'gx', split_axis=2, concat_axis=1, tiled=True)  6.11 us
    dynamic_slice x16, local copies, waits for them, and re-layouts, plane_histogram(): lax.scan(accumulate_plane, jnp.zeros((HISTOGRAM_BINS, HISTOGRAM_BINS), jn...  6 us
    dot_general x8, matrix products, accumulate_plane(): jnp.dot(dilatation_table, vorticity_table, precision=lax.Precision.HIGHEST)  4.61 us
  transfers between devices with their start and end apart: 7, of which 1 were waited for; matrix products, arithmetic and copies ran while one was open for 14% of the time, Pallas kernels for 0%

commit v1 on v0

--- a/solution.py
+++ b/solution.py
@@ -184,7 +184,8 @@
     back_lines = lax.all_to_all(returned, "gx", split_axis=1, concat_axis=2, tiled=True)
     conserved_next = back_lines.reshape(5, cells_x, span, cells_y)
     partial_histogram = plane_histogram(shock_sensor, dilatation_bin, vorticity_bin)
-    summed = lax.psum(partial_histogram, ("gx", "gy"))
+    half = lax.psum(partial_histogram, "gy")
+    summed = lax.psum(half, "gx")
     all_cells = cells_x * slab_count * span * total_y
     histogram = summed * (HISTOGRAM_BINS * HISTOGRAM_BINS / all_cells)
     return (conserved_next, histogram)

time: 218 us -> 258 us (1.18)
  blocking collectives: 116 us -> 156 us
    psum x1 -> x2, blocking collectives: 40.8 us -> 80.5 us  [the longest x1 77.1 us: shards(): summed = lax.psum(half, 'gx')]
  transfers between devices with their start and end apart: 7 -> 7, of which waited for: 1 -> 1; matrix products, arithmetic and copies ran while one was open for 14% -> 12% of each run, Pallas kernels for 0% -> 0%
where the time goes in v1:
time: 258 us; the launch traced here: 256 us
  blocking collectives  156 us (60%)
  local copies, waits for them, and re-layouts  39.8 us (15%)
  starting transfers between devices  25 us (10%)
  other arithmetic  22.1 us (9%)
  waiting for transfers between devices  6.05 us (2%)
  matrix products  5.56 us (2%)
    psum x1, blocking collectives, shards(): summed = lax.psum(half, 'gx')  77.1 us
    psum x1, blocking collectives, shards(): inflow = lax.psum(partial_sum, 'gx')  75.6 us
    unnamed x16, local copies, waits for them, and re-layouts  9.81 us
    ppermute x2, starting transfers between devices, extended(): before = lax.ppermute(last, axis, up)  8.5 us
    all_to_all x1, starting transfers between devices, shards(): lax.all_to_all(stacked, 'gx', split_axis=2, concat_axis=1, tiled=True)  6.88 us
    all_to_all x1, waiting for transfers between devices, shards(): lax.all_to_all(stacked, 'gx', split_axis=2, concat_axis=1, tiled=True)  6.04 us
    dynamic_slice x16, local copies, waits for them, and re-layouts, plane_histogram(): lax.scan(accumulate_plane, jnp.zeros((HISTOGRAM_BINS, HISTOGRAM_BINS), jn...  6 us
  transfers between devices with their start and end apart: 7, of which 1 were waited for; matrix products, arithmetic and copies ran while one was open for 12% of the time, Pallas kernels for 0%

profile of v1, /device:TPU:0, one launch (start us, length us, event | category | flops | bytes accessed | tf_op | source)
XLA Modules:
  0.0 256.0 jit_solution(4723747580588940098)
XLA Ops:
  0.6 0.9 pad_maximum_fusion.4
  1.6 1.3 collective-permute-start.1
  2.9 5.5 %collective-permute-start = (f32[5,1,32,32]{3,2,0,1:T(8,128)S(1)}, f32[5,1,32,32]{3,2,0,1:T(8,128)S(1)}, u32[]{:S(2)}, u32[]{:S(2)}) collective-permute-start(f32[5,1,32,32]{3,2,0,1:T(8,128)S(1)} %get-tuple-element.222), channel_id=1, source_target_pairs={{0,2},{2,4},{4,6},{6,8},{8,10},{10,12},{12,14},{14,16},{16,18},{18... | collective-permute-start | bytes 61448 | tf_op jit(solution)/shard_map/ppermute | solution.py:23
  8.4 0.7 convert_element_type.33
  9.1 0.7 convert_element_type.31
  9.7 0.7 multiply_multiply_fusion
  10.8 75.6 %psum.21 = f32[3,32,32]{2,1,0:T(8,128)S(1)} all-reduce(f32[3,32,32]{2,1,0:T(8,128)S(1)} %fusion.50), channel_id=1, replica_groups=mesh['gx'=16,'gy'=2] {'gx'}, use_global_device_ids=true, to_apply=%region_1.2 | all-reduce | flops 3072 | bytes 24576 | tf_op jit(solution)/shard_map/psum | solution.py:153
  86.4 1.2 pad_maximum_fusion.2
  87.6 0.7 convert_bitcast_fusion
  88.4 0.6 slice.495
  88.9 1.2 pad_maximum_fusion
  91.2 1.3 collective-permute-start.3
  92.5 3.0 %collective-permute-start.2 = (f32[5,10,32,1]{2,3,1,0:T(1,128)S(1)}, f32[5,10,32,1]{2,3,1,0:T(1,128)S(1)}, u32[]{:S(2)}, u32[]{:S(2)}) collective-permute-start(f32[5,10,32,1]{2,3,1,0:T(1,128)S(1)} %copy.81), channel_id=1, source_target_pairs={{0,1},{2,3},{4,5},{6,7},{8,9},{10,11},{12,13},{14,15},{16,17},{18,... | collective-permute-start | bytes 19208 | tf_op jit(solution)/shard_map/ppermute | solution.py:23
  95.5 1.4 and_reduce_fusion
  97.3 1.3 copy.84
  98.6 1.6 pad_maximum_fusion.1
  100.2 1.4 fusion.48
  101.6 1.7 scatter.14
  103.4 1.0 scatter.15
  104.5 0.9 scatter.16
  105.4 0.4 slice_select_fusion
  105.9 3.7 %scatter.19 = f32[5,10,32,34]{3,2,0,1:T(8,128)S(1)} dynamic-update-slice(f32[5,10,32,34]{3,2,0,1:T(8,128)S(1)} %scatter.16, f32[5,8,32,1]{3,2,0,1:T(8,128)S(1)} %slice_select_fusion, s32[]{:T(128)} %constant.328.clone.1, s32[]{:T(128)} %constant.350.clone.1, s32[]{:T(128)} %constant.328.clone.1, s32[]{:T(128)} %constant.351.clone.1) | dynamic-update-slice | bytes 10244 | tf_op jit(solution)/shard_map/scatter | solution.py:165
  111.2 1.2 fusion.91
  112.4 0.4 broadcast_multiply_fusion.3
  112.8 1.0 copy.119
  113.9 0.6 broadcast.273
  114.4 3.8 %reduce.27 = f32[1024,8]{1,0:T(8,128)} reduce(f32[1024,1,8]{2,1,0:T(1,128)} %bitcast.128, f32[]{:T(128)} %broadcast.273), dimensions={1}, to_apply=%bitcast.110.reduce_sub_computation | reduce | bytes 65540
  118.2 1.9 reshape.467
  120.1 3.5 %all-to-all-start.1 = ((f32[16,1,512]{2,1,0:T(1,128)}), f32[16,1,512]{2,1,0:T(1,128)S(1)}, u32[]{:S(2)}, u32[]{:S(2)}) async-start(f32[16,1,512]{2,1,0:T(1,128)} %reshape.467), calls=%async_computation.1 | async-start | bytes 65536 | tf_op jit(solution)/shard_map/all_to_all | solution.py:180
  123.6 2.7 %fusion.14 = f32[5,8,32,32]{3,2,0,1:T(8,128)} fusion(f32[5,10,32,34]{3,2,0,1:T(8,128)S(1)} %get-tuple-element.221, f32[5,10,32,34]{3,2,0,1:T(8,128)S(1)} %scatter.19, f32[5,8,1,32]{3,2,0,1:T(1,128)S(1)} %get-tuple-element.213, f32[5,8,31,32]{3,2,0,1:T(8,128)} %get-tuple-element.215, f32[5,8,31,32]{3,2,0,1:T(8,128)S(1)} %get-tuple-element.214, ...), kind=kLoop, calls=%fused_computation.23 | loop fusion | flops 368640 | bytes 4295680 | tf_op jit(solution)/shard_map/sub | solution.py:75
  126.3 3.6 %copy.122 = f32[5,8,32,32]{1,0,3,2:T(8,128)} copy(f32[5,8,32,32]{3,2,0,1:T(8,128)} %fusion.14) | data formatting | bytes 327680 | tf_op jit(solution)/shard_map/reshape | solution.py:176
  129.9 3.4 %reshape.465 = f32[16,1,2560]{2,1,0:T(1,128)} reshape(f32[1024,5,8]{2,1,0:T(8,128)} %bitcast.117) | data formatting | bytes 327680
  133.3 6.9 %all-to-all-start = ((f32[16,1,2560]{2,1,0:T(1,128)}), f32[16,1,2560]{2,1,0:T(1,128)S(1)}, u32[]{:S(2)}, u32[]{:S(2)}) async-start(f32[16,1,2560]{2,1,0:T(1,128)} %reshape.465), calls=%async_computation | async-start | bytes 327680 | tf_op jit(solution)/shard_map/all_to_all | solution.py:179
  140.2 0.7 reduce.28
  140.9 0.9 reshape.468
  142.1 6.0 %all-to-all-done = f32[16,1,2560]{2,1,0:T(1,128)S(1)} async-done(((f32[16,1,2560]{2,1,0:T(1,128)}), f32[16,1,2560]{2,1,0:T(1,128)S(1)}, u32[]{:S(2)}, u32[]{:S(2)}) %all-to-all-start) | async-done | bytes 163872 | tf_op jit(solution)/shard_map/all_to_all | solution.py:179
  148.1 1.0 reduce.26
  149.1 2.6 %reshape.466 = f32[1024,5,8]{2,1,0:T(8,128)} reshape(f32[16,2560]{1,0:T(8,128)S(1)} %reduce.26) | data formatting | bytes 327680
  151.7 2.6 %copy.103 = f32[5,16,8,64]{3,2,1,0:T(8,128)S(1)} copy(f32[5,16,8,64]{2,0,3,1:T(8,128)} %bitcast.118) | data formatting | bytes 327680 | tf_op jit(solution)/shard_map/all_to_all | solution.py:179
  154.5 0.7 fusion.10
  155.4 0.9 reshape.469
  156.3 3.5 %all-to-all-start.2 = ((f32[16,1,2560]{2,1,0:T(1,128)}), f32[16,1,2560]{2,1,0:T(1,128)S(1)}, u32[]{:S(2)}, u32[]{:S(2)}) async-start(f32[16,1,2560]{2,1,0:T(1,128)} %reshape.469), calls=%async_computation.2 | async-start | bytes 327680 | tf_op jit(solution)/shard_map/all_to_all | solution.py:184
  159.8 12.6 %while.22 = (s32[]{:T(128)}, f32[64,64]{1,0:T(8,128)S(1)}, s32[8,32,32]{2,1,0:T(8,128)}, s32[8,32,32]{2,1,0:T(8,128)}, f32[8,32,32]{2,1,0:T(8,128)S(1)}, /*index=5*/s32[]{:T(128)}, s32[]{:T(128)}) while((s32[]{:T(128)}, f32[64,64]{1,0:T(8,128)S(1)}, s32[8,32,32]{2,1,0:T(8,128)}, s32[8,32,32]{2,1,0:T(8,128)}, ...), condition=%wide.region_4.5_spmd.clone.clone, body=%wide.region_3.4_spmd.clone.clone.sunk | while | flops 50536448 | bytes 94311 | solution.py:113
  159.9 0.7 constant_dynamic-slice_fusion.6
  160.8 0.6 convolution_add_fusion.2
  161.5 0.7 constant_dynamic-slice_fusion.6
  162.4 0.6 convolution_add_fusion.2
  163.1 0.7 constant_dynamic-slice_fusion.6
  164.0 0.6 convolution_add_fusion.2
  164.6 0.7 constant_dynamic-slice_fusion.6
  165.5 0.6 convolution_add_fusion.2
  166.2 0.7 constant_dynamic-slice_fusion.6
  167.1 0.6 convolution_add_fusion.2
  167.8 0.7 constant_dynamic-slice_fusion.6
  168.7 0.6 convolution_add_fusion.2
  169.4 0.7 constant_dynamic-slice_fusion.6
  170.3 0.6 convolution_add_fusion.2
  170.9 0.7 constant_dynamic-slice_fusion.6
  171.8 0.6 convolution_add_fusion.2
  172.4 3.4 %psum.22 = f32[64,64]{1,0:T(8,128)S(1)} all-reduce(f32[64,64]{1,0:T(8,128)S(1)} %get-tuple-element.157), channel_id=1, replica_groups=mesh['gx'=16,'gy'=2] {'gy'}, use_global_device_ids=true, to_apply=%region_5.6 | all-reduce | flops 4096 | bytes 32768 | tf_op jit(solution)/shard_map/psum | solution.py:187
  175.8 77.1 %psum.23 = f32[64,64]{1,0:T(8,128)S(1)} all-reduce(f32[64,64]{1,0:T(8,128)S(1)} %psum.22), channel_id=1, replica_groups=mesh['gx'=16,'gy'=2] {'gx'}, use_global_device_ids=true, to_apply=%region_6.7 | all-reduce | flops 4096 | bytes 32768 | tf_op jit(solution)/shard_map/psum | solution.py:188
  252.9 0.6 broadcast_multiply_fusion.4
  253.6 1.0 reduce.29
  254.9 1.0 reshape.460
  (86 shorter events, 6.4 us)
Async XLA Ops:
  0.6 153.8 %copy-start = (f32[1,128,128]{2,1,0:T(8,128)S(1)}, f32[1,128,128]{2,1,0:T(8,128)}, u32[]{:S(2)}) copy-start(f32[1,128,128]{2,1,0:T(8,128)} %param.40) | copy-start | bytes 196612
  1.6 93.9 %copy-start.4 = (s32[4]{0:T(128)S(1)}, s32[4]{0:T(128)}, u32[]{:S(2)}) copy-start(s32[4]{0:T(128)} %constant.330.clone.1) | copy-start | bytes 52
  1.6 87.3 %collective-permute-start.1 = (f32[5,1,32,32]{3,2,0,1:T(8,128)S(1)}, f32[5,1,32,32]{3,2,0,1:T(8,128)S(1)}, u32[]{:S(2)}, u32[]{:S(2)}) collective-permute-start(f32[5,1,32,32]{3,2,0,1:T(8,128)S(1)} %get-tuple-element.223), channel_id=1, source_target_pairs={{2,0},{4,2},{6,4},{8,6},{10,8},{12,10},{14,12},{16,14},{18,16},{20... | collective-permute-start | bytes 61448 | tf_op jit(solution)/shard_map/ppermute | solution.py:24
  2.9 86.0 %collective-permute-start = (f32[5,1,32,32]{3,2,0,1:T(8,128)S(1)}, f32[5,1,32,32]{3,2,0,1:T(8,128)S(1)}, u32[]{:S(2)}, u32[]{:S(2)}) collective-permute-start(f32[5,1,32,32]{3,2,0,1:T(8,128)S(1)} %get-tuple-element.222), channel_id=1, source_target_pairs={{0,2},{2,4},{4,6},{6,8},{8,10},{10,12},{12,14},{14,16},{16,18},{18... | collective-permute-start | bytes 61448 | tf_op jit(solution)/shard_map/ppermute | solution.py:23
  87.6 11.0 %copy-start.1 = (f32[3,8,32,32]{3,2,1,0:T(8,128)S(1)}, f32[3,8,32,32]{3,2,1,0:T(8,128)}, u32[]{:S(2)}) copy-start(f32[3,8,32,32]{3,2,1,0:T(8,128)} %param.34) | copy-start | bytes 294916
  87.6 11.0 %copy-start.2 = (f32[8,32,32]{2,1,0:T(8,128)S(1)}, f32[8,32,32]{2,1,0:T(8,128)}, u32[]{:S(2)}) copy-start(f32[8,32,32]{2,1,0:T(8,128)} %param.35) | copy-start | bytes 98308
  87.6 11.0 %copy-start.3 = (f32[8,32,32]{2,1,0:T(8,128)S(1)}, f32[8,32,32]{2,1,0:T(8,128)}, u32[]{:S(2)}) copy-start(f32[8,32,32]{2,1,0:T(8,128)} %param.33) | copy-start | bytes 98308
  91.2 6.1 %collective-permute-start.3 = (f32[5,10,32,1]{2,3,1,0:T(1,128)S(1)}, f32[5,10,32,1]{2,3,1,0:T(1,128)S(1)}, u32[]{:S(2)}, u32[]{:S(2)}) collective-permute-start(f32[5,10,32,1]{2,3,1,0:T(1,128)S(1)} %copy.82), channel_id=1, source_target_pairs={{1,0},{3,2},{5,4},{7,6},{9,8},{11,10},{13,12},{15,14},{17,16},{19,... | collective-permute-start | bytes 19208 | tf_op jit(solution)/shard_map/ppermute | solution.py:24
  92.5 4.4 %collective-permute-start.2 = (f32[5,10,32,1]{2,3,1,0:T(1,128)S(1)}, f32[5,10,32,1]{2,3,1,0:T(1,128)S(1)}, u32[]{:S(2)}, u32[]{:S(2)}) collective-permute-start(f32[5,10,32,1]{2,3,1,0:T(1,128)S(1)} %copy.81), channel_id=1, source_target_pairs={{0,1},{2,3},{4,5},{6,7},{8,9},{10,11},{12,13},{14,15},{16,17},{18,... | collective-permute-start | bytes 19208 | tf_op jit(solution)/shard_map/ppermute | solution.py:23
  120.1 13.2 %all-to-all-start.1 = ((f32[16,1,512]{2,1,0:T(1,128)}), f32[16,1,512]{2,1,0:T(1,128)S(1)}, u32[]{:S(2)}, u32[]{:S(2)}) async-start(f32[16,1,512]{2,1,0:T(1,128)} %reshape.467), calls=%async_computation.1 | async-start | bytes 65536 | tf_op jit(solution)/shard_map/all_to_all | solution.py:180
  133.3 14.8 %all-to-all-start = ((f32[16,1,2560]{2,1,0:T(1,128)}), f32[16,1,2560]{2,1,0:T(1,128)S(1)}, u32[]{:S(2)}, u32[]{:S(2)}) async-start(f32[16,1,2560]{2,1,0:T(1,128)} %reshape.465), calls=%async_computation | async-start | bytes 327680 | tf_op jit(solution)/shard_map/all_to_all | solution.py:179
  156.3 97.3 %all-to-all-start.2 = ((f32[16,1,2560]{2,1,0:T(1,128)}), f32[16,1,2560]{2,1,0:T(1,128)S(1)}, u32[]{:S(2)}, u32[]{:S(2)}) async-start(f32[16,1,2560]{2,1,0:T(1,128)} %reshape.469), calls=%async_computation.2 | async-start | bytes 327680 | tf_op jit(solution)/shard_map/all_to_all | solution.py:184
